TPU v7x, 256 devices: a whole 4x4x8 slice. The times are simulated.
256 devices in a mesh: row: 16 (over z, core), col: 16 (over y, x).
Axes of the slice: x: 4, y: 4, z: 8, core: 2. Of those that a mesh axis runs over, the one named last changes fastest.
Arguments:
- tiles: bfloat16 [16, 16, 16, 512, 512], P('row', 'col'), as said below
- tile_rows: int32 [16, 16, 16], P('row', 'col'), may hold values from 0 to 11, as said below
- tile_cols: int32 [16, 16, 16], P('row', 'col'), may hold values from 0 to 11
- tile_counts: int32 [16, 16], P('row', 'col'), may hold values from 4 to 16, as said below
- sketch: bfloat16 [98304, 256], P(('row', 'col')), as said below
Outputs:
- basis: float32 [98304, 256], P(('row', 'col'))
- factor: float32 [256, 256], replicated
Inputs may be any that keep to these rules, and one draw needn't show every extreme that they name: Within one device's slots the pairs (tile_rows, tile_cols) are all different. `tile_counts`: some device uses all 16 slots in every draw. `tiles`: real valued tile entries of order one over the square root of a row's fan-in. `sketch`: real valued entries of order one.
All inputs are finite; a program needn't handle non-finite values.
Results may differ from a plain program's by a relative error of at most 0.0023.
Values may be sent and summed in bfloat16 or wider, within the bound.
A program may use at most 64 MiB of HBM per device.

v0:
```python
import jax
import jax.numpy as jnp
from jax import lax
from jax.sharding import PartitionSpec as P

BR = 12
BC = 12


def body(tiles, tile_rows, tile_cols, tile_counts, sketch):
    tile_size = tiles.shape[-1]
    sketch_width = sketch.shape[1]
    local_tiles = tiles[0, 0]
    row_ids = tile_rows[0, 0]
    col_ids = tile_cols[0, 0]
    live_count = tile_counts[0, 0]
    gathered = lax.all_gather(sketch, "col", axis=0, tiled=True)

    def transposed_step(slot_index, running):
        matrix = lax.dynamic_index_in_dim(local_tiles, slot_index, 0, keepdims=False)
        sketch_block = lax.dynamic_slice_in_dim(
            gathered, row_ids[slot_index] * tile_size, tile_size, 0
        )
        product = lax.dot_general(
            matrix, sketch_block, (((0,), (0,)), ((), ())), preferred_element_type=jnp.float32
        )
        target = col_ids[slot_index] * tile_size
        current = lax.dynamic_slice_in_dim(running, target, tile_size, 0)
        return lax.dynamic_update_slice_in_dim(running, current + product, target, 0)

    partial_cols = lax.fori_loop(
        0, live_count, transposed_step, jnp.zeros((BC * tile_size, sketch_width), jnp.float32)
    )
    shared = lax.psum_scatter(partial_cols, "row", scatter_dimension=0, tiled=True).astype(
        jnp.bfloat16
    )
    columns = lax.all_gather(shared, "row", axis=0, tiled=True)

    def forward_step(slot_index, running):
        matrix = lax.dynamic_index_in_dim(local_tiles, slot_index, 0, keepdims=False)
        column_block = lax.dynamic_slice_in_dim(
            columns, col_ids[slot_index] * tile_size, tile_size, 0
        )
        product = jnp.dot(matrix, column_block, preferred_element_type=jnp.float32)
        target = row_ids[slot_index] * tile_size
        current = lax.dynamic_slice_in_dim(running, target, tile_size, 0)
        return lax.dynamic_update_slice_in_dim(running, current + product, target, 0)

    partial_rows = lax.fori_loop(
        0, live_count, forward_step, jnp.zeros((BR * tile_size, sketch_width), jnp.float32)
    )
    owned_rows = lax.psum_scatter(partial_rows, "col", scatter_dimension=0, tiled=True)
    total_rows = BR * tile_size * lax.axis_size("row")
    local_gram = jnp.dot(
        owned_rows.T,
        owned_rows,
        precision=lax.Precision.HIGHEST,
        preferred_element_type=jnp.float32,
    )
    gram_matrix = lax.psum(local_gram, ("row", "col")) / total_rows
    cholesky_lower = jnp.linalg.cholesky(gram_matrix)
    basis_rows = lax.linalg.triangular_solve(
        cholesky_lower, owned_rows, left_side=False, lower=True, transpose_a=True
    )
    return (basis_rows, cholesky_lower.T)


def solution(mesh):
    return jax.shard_map(
        body,
        mesh=mesh,
        in_specs=(
            P("row", "col", None, None, None),
            P("row", "col", None),
            P("row", "col", None),
            P("row", "col"),
            P(("row", "col"), None),
        ),
        out_specs=(P(("row", "col"), None), P()),
        check_vma=False,
    )
```

profile of v0, /device:TPU:2, one launch (start us, length us, event | category | flops | bytes accessed | tf_op | source)
XLA Modules:
  0.0 780.2 jit_solution(2374643312332918244)
XLA Ops:
  8.0 57.3 %all-gather.3.cloned.1.call-done = bf16[6144,256]{1,0:T(8,128)(2,1)} async-done(((bf16[384,256]{1,0:T(8,128)(2,1)}), bf16[6144,256]{1,0:T(8,128)(2,1)}) %all-gather.3.cloned.1.call-update) | async-done | bytes 3145744 | tf_op jit(solution)/shard_map/all_gather | solution.py:17
  65.2 3.1 broadcast.98.clone
  68.3 47.2 %while.21 = (s32[]{:T(128)}, f32[6144,256]{1,0:T(8,128)}, s32[]{:T(128)}, s32[16]{0:T(128)S(1)}, bf16[16,512,512]{2,1,0:T(8,128)(2,1)}, /*index=5*/s32[16]{0:T(1...) while((s32[]{:T(128)}, f32[6144,256]{1,0:T(8,128)}, ...), condition=%wide.region_1.2_spmd, body=%wide.region_0.1_spmd.sunk | while | flops 134348816 | bytes 1835287 | solution.py:31
  71.7 2.4 fusion.37
  77.5 2.4 fusion.37
  83.3 2.4 fusion.37
  89.1 2.4 fusion.37
  95.0 2.4 fusion.37
  100.8 2.4 fusion.37
  106.6 2.4 fusion.37
  112.4 2.4 fusion.37
  115.6 113.3 %reduce-scatter.3.cloned.1.call-done = f32[384,256]{1,0:T(8,128)} async-done(((f32[6144,256]{1,0:T(8,128)}), f32[384,256]{1,0:T(8,128)}) %reduce-scatter.3.cloned.1.call-update) | async-done | bytes 393232 | tf_op jit(solution)/shard_map/reduce_scatter | solution.py:34
  228.9 1.7 convert_element_type.3
  230.6 39.8 %all-gather.5.cloned.1.call-done = bf16[6144,256]{1,0:T(8,128)(2,1)} async-done(((bf16[384,256]{1,0:T(8,128)(2,1)}), bf16[6144,256]{1,0:T(8,128)(2,1)}) %all-gather.5.cloned.1.call-update) | async-done | bytes 3145744 | tf_op jit(solution)/shard_map/all_gather | solution.py:37
  270.4 3.1 broadcast.98
  273.5 45.0 %while.22 = (s32[]{:T(128)}, f32[6144,256]{1,0:T(8,128)}, s32[]{:T(128)}, s32[16]{0:T(128)S(1)}, bf16[16,512,512]{2,1,0:T(8,128)(2,1)}, /*index=5*/s32[16]{0:T(1...) while((s32[]{:T(128)}, f32[6144,256]{1,0:T(8,128)}, ...), condition=%wide.region_4.5_spmd, body=%wide.region_3.4_spmd.sunk | while | flops 134348816 | bytes 1835287 | solution.py:49
  276.6 2.4 fusion.40
  282.2 2.4 fusion.40
  287.7 2.4 fusion.40
  293.3 2.4 fusion.40
  298.8 2.4 fusion.40
  304.4 2.4 fusion.40
  309.9 2.4 fusion.40
  315.5 2.4 fusion.40
  318.6 129.1 %reduce-scatter.5.cloned.1.call-done = f32[384,256]{1,0:T(8,128)} async-done(((f32[6144,256]{1,0:T(8,128)}), f32[384,256]{1,0:T(8,128)}) %reduce-scatter.5.cloned.1.call-update) | async-done | bytes 393232 | tf_op jit(solution)/shard_map/reduce_scatter | solution.py:52
  447.6 2.7 fusion.21
  450.4 257.2 %all-reduce.3.cloned.1.call-done = f32[256,256]{0,1:T(8,128)} async-done(((f32[256,256]{0,1:T(8,128)}), f32[256,256]{0,1:T(8,128)}) %all-reduce.3.cloned.1.call-update) | async-done | bytes 262160 | tf_op jit(solution)/shard_map/psum | solution.py:60
  709.7 11.7 %cholesky.50 = f32[128,128]{1,0:T(8,128)S(1)} custom-call(f32[128,128]{1,0:T(8,128)S(1)} %cholesky.118), custom_call_target="Cholesky" | custom-call | tf_op jit(solution)/shard_map/jit(cholesky)/cholesky | solution.py:61
  721.5 9.8 %custom-call.14 = f32[1,128,128]{1,2,0:T(8,128)S(1)} custom-call(f32[1,128,128]{2,1,0:T(8,128)S(1)} %get-tuple-element.133), custom_call_target="InvertDiagBlocksLowerTriangular" | custom-call | tf_op jit(solution)/shard_map/jit(cholesky)/cholesky | solution.py:61
  731.8 11.7 %cholesky.105 = f32[128,128]{1,0:T(8,128)S(1)} custom-call(f32[128,128]{1,0:T(8,128)S(1)} %convolution_subtract_fusion.1), custom_call_target="Cholesky" | custom-call | tf_op jit(solution)/shard_map/jit(cholesky)/cholesky | solution.py:61
  745.7 4.2 while.23
  750.0 19.7 %custom-call.15 = f32[2,128,128]{1,2,0:T(8,128)S(1)} custom-call(f32[2,128,128]{2,1,0:T(8,128)S(1)} %get-tuple-element.87), custom_call_target="InvertDiagBlocksLowerTriangular" | custom-call | tf_op jit(solution)/shard_map/triangular_solve | solution.py:62
  (74 shorter events, 32.5 us)
Async XLA Ops:
  7.2 61.1 %copy-start.2 = (s32[1,1,16]{2,1,0:T(1,128)S(1)}, s32[1,1,16]{2,1,0:T(1,128)}, u32[]{:S(2)}) copy-start(s32[1,1,16]{2,1,0:T(1,128)} %param.10) | copy-start | bytes 196
  7.2 61.1 %copy-start.1 = (s32[1,1,16]{2,1,0:T(1,128)S(1)}, s32[1,1,16]{2,1,0:T(1,128)}, u32[]{:S(2)}) copy-start(s32[1,1,16]{2,1,0:T(1,128)} %param.11) | copy-start | bytes 196
  7.2 58.0 %all-gather.3.cloned.1.call-start = ((), (), s32[]{:S(2)}) async-start(), calls=%async_computation.2 | async-start | bytes 3342336 | tf_op jit(solution)/shard_map/all_gather | solution.py:17
  7.9 220.9 %reduce-scatter.3.cloned.1.call-start = ((), (), s32[]{:S(2)}) async-start(), calls=%async_computation.3 | async-start | bytes 6684672 | tf_op jit(solution)/shard_map/reduce_scatter | solution.py:34
  115.5 154.9 %all-gather.5.cloned.1.call-start = ((), (), s32[]{:S(2)}) async-start(), calls=%async_computation.4 | async-start | bytes 3342336 | tf_op jit(solution)/shard_map/all_gather | solution.py:37
  230.6 217.1 %reduce-scatter.5.cloned.1.call-start = ((), (), s32[]{:S(2)}) async-start(), calls=%async_computation.5 | async-start | bytes 6684672 | tf_op jit(solution)/shard_map/reduce_scatter | solution.py:52
  318.5 389.1 %all-reduce.3.cloned.1.call-start = ((), (), s32[]{:S(2)}) async-start(), calls=%async_computation.6 | async-start | bytes 524288 | tf_op jit(solution)/shard_map/psum | solution.py:60
  447.6 323.4 %copy-start = (f32[384,256]{1,0:T(8,128)S(1)}, f32[384,256]{1,0:T(8,128)}, u32[]{:S(2)}) copy-start(f32[384,256]{1,0:T(8,128)} %reduce-scatter.5.cloned.1.call-done) | copy-start | bytes 1179652
Sparse Core Ops, SparseCore 0:
  10.4 54.7 all-gather.2
  115.7 113.1 reduce-scatter.2
  231.3 39.0 all-gather.4
  318.6 128.9 reduce-scatter.4
  453.5 254.0 all-reduce.2
where the time goes:
time: 782 us; the launch traced here: 780 us
  waiting for transfers between devices  597 us (76%)
  other arithmetic  57.4 us (7%)
  matrix products  44 us (6%)
  loops' own time  33.8 us (4%)
  local copies, waits for them, and re-layouts  32.2 us (4%)
  between operations  15.3 us (2%)
    psum x1, waiting for transfers between devices, body(): gram_matrix = lax.psum(local_gram, ('row', 'col')) / total_rows  257 us
    reduce_scatter x1, waiting for transfers between devices, body(): lax.psum_scatter(partial_rows, 'col', scatter_dimension=0, tiled=True)  129 us
    reduce_scatter x1, waiting for transfers between devices, body(): lax.psum_scatter(partial_cols, 'row', scatter_dimension=0, tiled=True)  113 us
    all_gather x1, waiting for transfers between devices, body(): gathered = lax.all_gather(sketch, 'col', axis=0, tiled=True)  57.3 us
    all_gather x1, waiting for transfers between devices, body(): columns = lax.all_gather(shared, 'row', axis=0, tiled=True)  39.8 us
    another operation x6, other arithmetic, body(): cholesky_lower = jnp.linalg.cholesky(gram_matrix)  34 us
    another operation x3, other arithmetic, body(): lax.linalg.triangular_solve(cholesky_lower, owned_rows, left_side=False,...  19.7 us
    dot_general x8, matrix products, transposed_step(): lax.dot_general(matrix, sketch_block, (((0,), (0,)), ((), ())), preferred...  19.4 us
  transfers between devices with their start and end apart: 5, of which 5 were waited for; matrix products, arithmetic and copies ran while one was open for 0% of the time, Pallas kernels for 0%

commit v1 on v0

--- a/solution.py
+++ b/solution.py
@@ -57,7 +57,7 @@
         precision=lax.Precision.HIGHEST,
         preferred_element_type=jnp.float32,
     )
-    gram_matrix = lax.psum(local_gram, ("row", "col")) / total_rows
+    gram_matrix = lax.psum(lax.psum(local_gram, "col"), "row") / total_rows
     cholesky_lower = jnp.linalg.cholesky(gram_matrix)
     basis_rows = lax.linalg.triangular_solve(
         cholesky_lower, owned_rows, left_side=False, lower=True, transpose_a=True

time: 782 us -> 733 us (0.937)
  waiting for transfers between devices: 597 us -> 547 us
    psum x1 -> x2, waiting for transfers between devices: 257 us -> 207 us  [body(): gram_matrix = lax.psum(lax.psum(local_gram, 'col'), 'row') / total_rows]
  transfers between devices with their start and end apart: 5 -> 6, of which waited for: 5 -> 6; matrix products, arithmetic and copies ran while one was open for 0% -> 0% of each run, Pallas kernels for 0% -> 0%
where the time goes in v1:
time: 733 us; the launch traced here: 730 us
  waiting for transfers between devices  547 us (75%)
  other arithmetic  57.4 us (8%)
  matrix products  43 us (6%)
  loops' own time  33.9 us (5%)
  local copies, waits for them, and re-layouts  32.2 us (4%)
  between operations  15.6 us (2%)
    psum x2, waiting for transfers between devices, body(): gram_matrix = lax.psum(lax.psum(local_gram, 'col'), 'row') / total_rows  207 us
    reduce_scatter x1, waiting for transfers between devices, body(): lax.psum_scatter(partial_rows, 'col', scatter_dimension=0, tiled=True)  129 us
    reduce_scatter x1, waiting for transfers between devices, body(): lax.psum_scatter(partial_cols, 'row', scatter_dimension=0, tiled=True)  113 us
    all_gather x1, waiting for transfers between devices, body(): gathered = lax.all_gather(sketch, 'col', axis=0, tiled=True)  57.3 us
    all_gather x1, waiting for transfers between devices, body(): columns = lax.all_gather(shared, 'row', axis=0, tiled=True)  39.8 us
    another operation x6, other arithmetic, body(): cholesky_lower = jnp.linalg.cholesky(gram_matrix)  34 us
    another operation x3, other arithmetic, body(): lax.linalg.triangular_solve(cholesky_lower, owned_rows, left_side=False,...  19.7 us
    dot_general x8, matrix products, transposed_step(): lax.dot_general(matrix, sketch_block, (((0,), (0,)), ((), ())), preferred...  19.4 us
  transfers between devices with their start and end apart: 6, of which 6 were waited for; matrix products, arithmetic and copies ran while one was open for 0% of the time, Pallas kernels for 0%

profile of v1, /device:TPU:2, one launch (start us, length us, event | category | flops | bytes accessed | tf_op | source)
XLA Modules:
  0.0 729.7 jit_solution(5545388819137194925)
XLA Ops:
  8.0 57.3 %all-gather.3.cloned.1.call-done = bf16[6144,256]{1,0:T(8,128)(2,1)} async-done(((bf16[384,256]{1,0:T(8,128)(2,1)}), bf16[6144,256]{1,0:T(8,128)(2,1)}) %all-gather.3.cloned.1.call-update) | async-done | bytes 3145744 | tf_op jit(solution)/shard_map/all_gather | solution.py:17
  65.2 3.1 broadcast.98.clone
  68.3 47.2 %while.21 = (s32[]{:T(128)}, f32[6144,256]{1,0:T(8,128)}, s32[]{:T(128)}, s32[16]{0:T(128)S(1)}, bf16[16,512,512]{2,1,0:T(8,128)(2,1)}, /*index=5*/s32[16]{0:T(1...) while((s32[]{:T(128)}, f32[6144,256]{1,0:T(8,128)}, ...), condition=%wide.region_1.2_spmd, body=%wide.region_0.1_spmd.sunk | while | flops 134348816 | bytes 1835287 | solution.py:31
  71.7 2.4 fusion.37
  77.5 2.4 fusion.37
  83.3 2.4 fusion.37
  89.1 2.4 fusion.37
  95.0 2.4 fusion.37
  100.8 2.4 fusion.37
  106.6 2.4 fusion.37
  112.4 2.4 fusion.37
  115.6 113.3 %reduce-scatter.3.cloned.1.call-done = f32[384,256]{1,0:T(8,128)} async-done(((f32[6144,256]{1,0:T(8,128)}), f32[384,256]{1,0:T(8,128)}) %reduce-scatter.3.cloned.1.call-update) | async-done | bytes 393232 | tf_op jit(solution)/shard_map/reduce_scatter | solution.py:34
  230.6 39.8 %all-gather.5.cloned.1.call-done = bf16[6144,256]{1,0:T(8,128)(2,1)} async-done(((bf16[384,256]{1,0:T(8,128)(2,1)}), bf16[6144,256]{1,0:T(8,128)(2,1)}) %all-gather.5.cloned.1.call-update) | async-done | bytes 3145744 | tf_op jit(solution)/shard_map/all_gather | solution.py:37
  270.4 3.1 broadcast.98
  273.5 45.0 %while.22 = (s32[]{:T(128)}, f32[6144,256]{1,0:T(8,128)}, s32[]{:T(128)}, s32[16]{0:T(128)S(1)}, bf16[16,512,512]{2,1,0:T(8,128)(2,1)}, /*index=5*/s32[16]{0:T(1...) while((s32[]{:T(128)}, f32[6144,256]{1,0:T(8,128)}, ...), condition=%wide.region_4.5_spmd, body=%wide.region_3.4_spmd.sunk | while | flops 134348816 | bytes 1835287 | solution.py:49
  276.6 2.4 fusion.40
  282.2 2.4 fusion.40
  287.7 2.4 fusion.40
  293.3 2.4 fusion.40
  298.8 2.4 fusion.40
  304.4 2.4 fusion.40
  309.9 2.4 fusion.40
  315.5 2.4 fusion.40
  318.6 129.1 %reduce-scatter.5.cloned.1.call-done = f32[384,256]{1,0:T(8,128)} async-done(((f32[6144,256]{1,0:T(8,128)}), f32[384,256]{1,0:T(8,128)}) %reduce-scatter.5.cloned.1.call-update) | async-done | bytes 393232 | tf_op jit(solution)/shard_map/reduce_scatter | solution.py:52
  447.6 2.7 fusion.21
  450.6 95.1 %all-reduce.4.cloned.1.call-done = f32[256,256]{0,1:T(8,128)} async-done(((f32[256,256]{0,1:T(8,128)}), f32[256,256]{0,1:T(8,128)}) %all-reduce.4.cloned.1.call-update) | async-done | bytes 262160 | tf_op jit(solution)/shard_map/psum | solution.py:60
  545.7 111.9 %all-reduce.6.cloned.1.call-done = f32[256,256]{0,1:T(8,128)} async-done(((f32[256,256]{0,1:T(8,128)}), f32[256,256]{0,1:T(8,128)}) %all-reduce.6.cloned.1.call-update) | async-done | bytes 262160 | tf_op jit(solution)/shard_map/psum | solution.py:60
  659.8 11.7 %cholesky.50 = f32[128,128]{1,0:T(8,128)S(1)} custom-call(f32[128,128]{1,0:T(8,128)S(1)} %cholesky.118), custom_call_target="Cholesky" | custom-call | tf_op jit(solution)/shard_map/jit(cholesky)/cholesky | solution.py:61
  671.5 9.8 %custom-call.14 = f32[1,128,128]{1,2,0:T(8,128)S(1)} custom-call(f32[1,128,128]{2,1,0:T(8,128)S(1)} %get-tuple-element.133), custom_call_target="InvertDiagBlocksLowerTriangular" | custom-call | tf_op jit(solution)/shard_map/jit(cholesky)/cholesky | solution.py:61
  681.8 11.7 %cholesky.105 = f32[128,128]{1,0:T(8,128)S(1)} custom-call(f32[128,128]{1,0:T(8,128)S(1)} %convolution_subtract_fusion.1), custom_call_target="Cholesky" | custom-call | tf_op jit(solution)/shard_map/jit(cholesky)/cholesky | solution.py:61
  695.8 4.3 while.23
  700.0 19.7 %custom-call.15 = f32[2,128,128]{1,2,0:T(8,128)S(1)} custom-call(f32[2,128,128]{2,1,0:T(8,128)S(1)} %get-tuple-element.87), custom_call_target="InvertDiagBlocksLowerTriangular" | custom-call | tf_op jit(solution)/shard_map/triangular_solve | solution.py:62
  (77 shorter events, 33.5 us)
Async XLA Ops:
  7.2 61.1 %copy-start.2 = (s32[1,1,16]{2,1,0:T(1,128)S(1)}, s32[1,1,16]{2,1,0:T(1,128)}, u32[]{:S(2)}) copy-start(s32[1,1,16]{2,1,0:T(1,128)} %param.10) | copy-start | bytes 196
  7.2 61.1 %copy-start.1 = (s32[1,1,16]{2,1,0:T(1,128)S(1)}, s32[1,1,16]{2,1,0:T(1,128)}, u32[]{:S(2)}) copy-start(s32[1,1,16]{2,1,0:T(1,128)} %param.11) | copy-start | bytes 196
  7.2 58.0 %all-gather.3.cloned.1.call-start = ((), (), s32[]{:S(2)}) async-start(), calls=%async_computation.2 | async-start | bytes 3342336 | tf_op jit(solution)/shard_map/all_gather | solution.py:17
  7.9 220.9 %reduce-scatter.3.cloned.1.call-start = ((), (), s32[]{:S(2)}) async-start(), calls=%async_computation.3 | async-start | bytes 6684672 | tf_op jit(solution)/shard_map/reduce_scatter | solution.py:34
  115.5 154.9 %all-gather.5.cloned.1.call-start = ((), (), s32[]{:S(2)}) async-start(), calls=%async_computation.4 | async-start | bytes 3342336 | tf_op jit(solution)/shard_map/all_gather | solution.py:37
  230.6 217.1 %reduce-scatter.5.cloned.1.call-start = ((), (), s32[]{:S(2)}) async-start(), calls=%async_computation.5 | async-start | bytes 6684672 | tf_op jit(solution)/shard_map/reduce_scatter | solution.py:52
  318.5 227.2 %all-reduce.4.cloned.1.call-start = ((), (), s32[]{:S(2)}) async-start(), calls=%async_computation.6 | async-start | bytes 524288 | tf_op jit(solution)/shard_map/psum | solution.py:60
  447.6 272.1 %copy-start = (f32[384,256]{1,0:T(8,128)S(1)}, f32[384,256]{1,0:T(8,128)}, u32[]{:S(2)}) copy-start(f32[384,256]{1,0:T(8,128)} %reduce-scatter.5.cloned.1.call-done) | copy-start | bytes 1179652
  450.4 207.3 %all-reduce.6.cloned.1.call-start = ((), (), s32[]{:S(2)}) async-start(), calls=%async_computation.7 | async-start | bytes 524288 | tf_op jit(solution)/shard_map/psum | solution.py:60
Sparse Core Ops, SparseCore 0:
  10.4 54.7 all-gather.2
  115.7 113.1 reduce-scatter.2
  231.3 39.0 all-gather.4
  318.6 128.9 reduce-scatter.4
  451.2 94.4 all-reduce.3
  547.9 109.7 all-reduce.5
